TPU v7x, 256 devices: a whole 4x4x8 slice. The times are simulated.
256 devices in a mesh: dp: 32 (over x, y, core), mp: 8 (over z).
Axes of the slice: x: 4, y: 4, z: 8, core: 2. Of those that a mesh axis runs over, the one named last changes fastest.
Arguments:
- features: bfloat16 [65536, 2, 512], P('dp'), may hold values from -27 to 27
- projection: bfloat16 [512, 256], replicated, may hold values from -1 to 1
- prototypes: float32 [3000, 256], P('mp'), may hold values from -7 to 7
Outputs:
- grad_prototypes: float32 [3000, 256], P('mp')
- grad_projection: float32 [512, 256], replicated
- loss: float32 [], replicated
All inputs are finite; a program needn't handle non-finite values.
Results may differ from a plain program's by a relative error of at most 0.0019.
The roundings to bfloat16 on the way count: a program that leaves them out, or rounds other values in their place, can miss the bound.
Values may be sent and summed in bfloat16 or wider, within the bound.
A program may use at most 128 MiB of HBM per device.

v0:
```python
import jax
import jax.numpy as jnp
from jax import lax
from jax.sharding import PartitionSpec as P

ITERS = 3
EPSILON_CODES = 0.05
SOFTMAX_TEMPER = 0.1
LOSS_FACTOR = 4096.0
TINY = 1e-06


def unit_rows(values):
    inverse = lax.rsqrt(jnp.sum(values * values, axis=-1, keepdims=True) + TINY)
    return (values * inverse, inverse)


def prototype_totals(values):
    return lax.psum(jnp.sum(values, axis=0), "dp")


def code_totals(values):
    return lax.psum(jnp.sum(values, axis=-1), "mp")


def loss_pieces(
    prototype_logits, softmax_exponent, softmax_denominator, assignments, gradient_factor
):
    swapped_targets = assignments[:, ::-1]
    grad_half = (
        (softmax_exponent / softmax_denominator[..., None] - swapped_targets) * gradient_factor
    ).astype(jnp.bfloat16)
    loss_portion = jnp.sum(
        swapped_targets
        * (prototype_logits * (1.0 / SOFTMAX_TEMPER) - jnp.log(softmax_denominator)[..., None])
    )
    return (grad_half, loss_portion)


def embed_backward(grad_unit, embed_unit, embed_inverse, own_feats):
    along_unit = jnp.sum(embed_unit * grad_unit, axis=-1, keepdims=True)
    grad_raw = ((grad_unit - embed_unit * along_unit) * embed_inverse).astype(jnp.bfloat16)
    return jnp.einsum("bve,bvp->ep", own_feats, grad_raw, preferred_element_type=jnp.float32)


def body(features, projection, prototypes):
    local_rows = features.shape[0]
    own_count = local_rows // lax.axis_size("mp")
    batch_row_count = local_rows * lax.axis_size("dp")
    gradient_factor = LOSS_FACTOR / (2.0 * batch_row_count * SOFTMAX_TEMPER)
    proto_unit, proto_inverse = unit_rows(prototypes)
    proto_half = proto_unit.astype(jnp.bfloat16)
    first_row = lax.axis_index("mp") * own_count
    own_feats = lax.dynamic_slice_in_dim(features, first_row, own_count, 0)
    raw_embed = jnp.einsum("bve,ep->bvp", own_feats, projection, preferred_element_type=jnp.float32)
    embed_unit, embed_inverse = unit_rows(raw_embed)
    embed_half = embed_unit.astype(jnp.bfloat16)
    all_embed = lax.all_gather(embed_half, "mp", axis=0, tiled=True)
    prototype_logits = jnp.einsum(
        "bvp,kp->bvk", all_embed, proto_half, preferred_element_type=jnp.float32
    )
    transport = jnp.exp(prototype_logits * (1.0 / EPSILON_CODES))
    softmax_exponent = jnp.exp(prototype_logits * (1.0 / SOFTMAX_TEMPER))
    soft_part = jnp.sum(softmax_exponent, axis=-1)
    for iteration in range(ITERS - 1):
        transport = transport / prototype_totals(transport)[None]
        transport = transport / code_totals(transport)[..., None]
    transport = transport / prototype_totals(transport)[None]
    softmax_denominator = lax.psum(soft_part, "mp")
    row_sums = code_totals(transport)
    assignments = transport / row_sums[..., None]
    grad_half, loss_portion = loss_pieces(
        prototype_logits, softmax_exponent, softmax_denominator, assignments, gradient_factor
    )
    proto_grad = jnp.einsum("bvk,bvp->kp", grad_half, all_embed, preferred_element_type=jnp.float32)
    proto_grad = lax.psum(proto_grad, "dp")
    grad_unit = lax.psum_scatter(
        jnp.einsum("bvk,kp->bvp", grad_half, proto_half, preferred_element_type=jnp.float32),
        "mp",
        scatter_dimension=0,
        tiled=True,
    )
    weight_part = embed_backward(grad_unit, embed_unit, embed_inverse, own_feats)
    weight_grad, loss_total = lax.psum((weight_part, loss_portion), ("dp", "mp"))
    along_proto = jnp.sum(proto_unit * proto_grad, axis=-1, keepdims=True)
    grad_protos = (proto_grad - proto_unit * along_proto) * proto_inverse
    loss_value = -loss_total / (2.0 * batch_row_count)
    return (grad_protos, weight_grad, loss_value)


def solution(mesh):
    return jax.shard_map(
        body,
        mesh=mesh,
        in_specs=(P("dp", None, None), P(), P("mp", None)),
        out_specs=(P("mp", None), P(), P()),
        check_vma=False,
    )
```

profile of v0, /device:TPU:2, one launch (start us, length us, event | category | flops | bytes accessed | tf_op | source)
XLA Modules:
  0.0 803.6 jit_solution(7048572155357733132)
XLA Ops:
  7.2 0.0 copy-start
  7.2 0.0 all-gather.2.cloned.1.call-start
  7.2 1.4 constant_dynamic-slice_fusion
  8.7 0.0 copy-start.3
  8.7 0.8 copy-done.3
  9.5 0.0 copy-done
  9.5 0.4 multiply_reduce_fusion.1
  9.9 0.7 multiply_convert_fusion.1
  10.6 0.0 all-gather.2.cloned.1.call-update
  10.6 0.0 reduce-scatter.2.cloned.1.call-start
  10.7 1.1 multiply_reduce_fusion.4
  11.8 49.1 %all-gather.2.cloned.1.call-done = bf16[2048,2,256]{0,2,1:T(8,128)(2,1)} async-done(((bf16[256,2,256]{0,2,1:T(8,128)(2,1)}), bf16[2048,2,256]{0,2,1:T(8,128)(2,1)}) %all-gather.2.cloned.1.call-update) | async-done | bytes 2097168 | tf_op jit(solution)/shard_map/all_gather | solution.py:58
  60.9 5.4 fusion.12
  66.3 53.0 %psum.71 = f32[2,375]{1,0:T(2,128)S(1)} all-reduce(f32[2,375]{1,0:T(2,128)S(1)} %get-tuple-element.11), channel_id=1, replica_groups=mesh['dp'=32,'mp'=8] {'dp'}, use_global_device_ids=true, to_apply=%region_5.0 | all-reduce | flops 750 | bytes 6000 | tf_op jit(solution)/shard_map/psum | solution.py:19
  119.3 3.8 exponential_reduce_fusion
  123.2 29.9 %psum.72 = f32[2048,2]{0,1:T(2,128)S(1)} all-reduce(f32[2048,2]{0,1:T(2,128)S(1)} %get-tuple-element.4), channel_id=1, replica_groups=mesh['dp'=32,'mp'=8] {'mp'}, use_global_device_ids=true, to_apply=%region_7.0 | all-reduce | flops 4096 | bytes 32768 | tf_op jit(solution)/shard_map/psum | solution.py:23
  153.0 4.4 fusion.8
  157.5 54.7 %psum.73 = f32[2,375]{1,0:T(2,128)S(1)} all-reduce(f32[2,375]{1,0:T(2,128)S(1)} %fusion.8), channel_id=1, replica_groups=mesh['dp'=32,'mp'=8] {'dp'}, use_global_device_ids=true, to_apply=%region_9.0 | all-reduce | flops 750 | bytes 6000 | tf_op jit(solution)/shard_map/psum | solution.py:19
  212.1 3.7 fusion.9
  215.9 27.0 %psum.74 = f32[2048,2]{0,1:T(2,128)S(1)} all-reduce(f32[2048,2]{0,1:T(2,128)S(1)} %fusion.9), channel_id=1, replica_groups=mesh['dp'=32,'mp'=8] {'mp'}, use_global_device_ids=true, to_apply=%region_11.0 | all-reduce | flops 4096 | bytes 32768 | tf_op jit(solution)/shard_map/psum | solution.py:23
  242.9 3.9 fusion.10
  246.8 62.7 %psum.75 = f32[2,375]{1,0:T(2,128)S(1)} all-reduce(f32[2,375]{1,0:T(2,128)S(1)} %fusion.10), channel_id=1, replica_groups=mesh['dp'=32,'mp'=8] {'dp'}, use_global_device_ids=true, to_apply=%region_13.0 | all-reduce | flops 750 | bytes 6000 | tf_op jit(solution)/shard_map/psum | solution.py:19
  309.5 0.0 slice-start
  309.5 4.3 fusion.11
  313.8 27.7 %all-reduce = (f32[2048,2]{0,1:T(2,128)S(1)}, f32[2048,2]{0,1:T(2,128)S(1)}) all-reduce(f32[2048,2]{0,1:T(2,128)S(1)} %fusion.11, f32[2048,2]{0,1:T(2,128)S(1)} %get-tuple-element.3), channel_id=1, replica_groups=mesh['dp'=32,'mp'=8] {'mp'}, use_global_device_ids=true, to_apply=%region_15.0 | all-reduce | flops 8192 | bytes 65536 | tf_op jit(solution)/shard_map/psum | solution.py:23
  341.5 0.0 slice-start.1
  341.5 5.1 fusion.7
  346.6 0.0 slice-done
  346.6 0.0 slice-done.1
  346.7 0.0 copy-start.2
  346.7 2.6 multiply_reduce_fusion
  349.2 0.0 copy-start.1
  349.2 1.6 copy-done.1
  350.9 0.0 copy-done.2
  350.9 3.3 fusion.28
  354.2 0.0 copy-start.4
  354.2 0.0 reduce-scatter.2.cloned.1.call-update
  354.2 0.0 all-reduce.4.cloned.1.call-start
  354.3 4.3 convolution_bitcast_fusion.1
  358.6 0.0 all-reduce.4.cloned.1.call-update
  358.7 0.0 all-reduce.6.cloned.1.call-start
  358.7 90.6 %psum.79 = f32[]{:T(128)} all-reduce(f32[]{:T(128)} %get-tuple-element.7), channel_id=1, replica_groups=mesh['dp'=32,'mp'=8] {'dp','mp'}, use_global_device_ids=true, to_apply=%region_22.0 | all-reduce | flops 1 | bytes 8 | tf_op jit(solution)/shard_map/psum | solution.py:84
  449.9 0.0 reduce-scatter.2.cloned.1.call-done
  450.0 0.0 copy-done.4
  450.0 2.5 convolution_bitcast_fusion
  452.5 0.0 all-reduce.6.cloned.1.call-update
  452.5 83.7 %all-reduce.4.cloned.1.call-done = f32[375,256]{1,0:T(8,128)} async-done(((f32[375,256]{1,0:T(8,128)}), f32[375,256]{1,0:T(8,128)}) %all-reduce.4.cloned.1.call-update) | async-done | bytes 384016 | tf_op jit(solution)/shard_map/psum | solution.py:76
  536.2 1.2 multiply_reduce_fusion.3
  537.4 1.9 subtract_multiply_fusion
  539.3 254.8 %all-reduce.6.cloned.1.call-done = f32[512,256]{1,0:T(8,128)} async-done(((f32[512,256]{1,0:T(8,128)}), f32[512,256]{1,0:T(8,128)}) %all-reduce.6.cloned.1.call-update) | async-done | bytes 524304 | tf_op jit(solution)/shard_map/psum | solution.py:84
  794.1 1.9 copy.29
  (4 shorter events, 0.0 us)
Async XLA Ops:
  7.2 2.3 copy-start
  7.2 53.7 %all-gather.2.cloned.1.call-start = ((), (), s32[]{:S(2)}) async-start(), calls=%async_computation.1 | async-start | bytes 2359296 | tf_op jit(solution)/shard_map/all_gather | solution.py:58
  8.7 0.8 copy-start.3
  10.6 439.3 %reduce-scatter.2.cloned.1.call-start = ((), (), s32[]{:S(2)}) async-start(), calls=%async_computation.3 | async-start | bytes 4718592 | tf_op jit(solution)/shard_map/reduce_scatter | solution.py:77
  309.5 37.1 %slice-start = ((s8[6160384]{0:T(1024)(128)(4,1)}), s8[1966080]{0:T(1024)(128)(4,1)S(1)}, s32[]{:S(2)}) async-start(s8[6160384]{0:T(1024)(128)(4,1)} %bitcast.19), calls=%async_computation.5 | async-start | bytes 3932160
  341.5 5.1 slice-start.1
  346.7 4.2 copy-start.2
  349.2 1.6 copy-start.1
  354.2 95.8 %copy-start.4 = (bf16[256,2,512]{2,1,0:T(2,128)(2,1)S(1)}, bf16[256,2,512]{2,1,0:T(2,128)(2,1)}, u32[]{:S(2)}) copy-start(bf16[256,2,512]{2,1,0:T(2,128)(2,1)} %copy-done.3) | copy-start | bytes 1572868
  354.2 181.9 %all-reduce.4.cloned.1.call-start = ((), (), s32[]{:S(2)}) async-start(), calls=%async_computation.2 | async-start | bytes 770048 | tf_op jit(solution)/shard_map/psum | solution.py:76
  358.7 435.4 %all-reduce.6.cloned.1.call-start = ((), (), s32[]{:S(2)}) async-start(), calls=%async_computation.4 | async-start | bytes 1048576 | tf_op jit(solution)/shard_map/psum | solution.py:84
Sparse Core Ops, SparseCore 0:
  10.7 50.1 all-gather.1
  354.4 66.9 reduce-scatter.1
  425.2 110.8 all-reduce.3
  542.1 251.9 all-reduce.5
where the time goes:
time: 804 us
  waiting for transfers between devices  388 us (48%)
  blocking collectives  345 us (43%)
  other arithmetic  32.9 us (4%)
  matrix products  16 us (2%)
  between operations  15.7 us (2%)
    psum x1, waiting for transfers between devices, body(): lax.psum((weight_part, loss_portion), ('dp', 'mp'))  255 us
    psum x3, blocking collectives, prototype_totals(): return lax.psum(jnp.sum(values, axis=0), 'dp')  170 us
    psum x1, blocking collectives, body(): lax.psum((weight_part, loss_portion), ('dp', 'mp'))  90.6 us
    psum x3, blocking collectives, code_totals(): return lax.psum(jnp.sum(values, axis=-1), 'mp')  84.6 us
    psum x1, waiting for transfers between devices, body(): proto_grad = lax.psum(proto_grad, 'dp')  83.7 us
    all_gather x1, waiting for transfers between devices, body(): all_embed = lax.all_gather(embed_half, 'mp', axis=0, tiled=True)  49.1 us
  transfers between devices with their start and end apart: 4, of which 3 were waited for; matrix products, arithmetic and copies ran while one was open for 1% of the time, Pallas kernels for 0%

commit v1 on v0

--- a/solution.py
+++ b/solution.py
@@ -81,7 +81,7 @@
         tiled=True,
     )
     weight_part = embed_backward(grad_unit, embed_unit, embed_inverse, own_feats)
-    weight_grad, loss_total = lax.psum((weight_part, loss_portion), ("dp", "mp"))
+    weight_grad, loss_total = lax.psum(lax.psum((weight_part, loss_portion), "mp"), "dp")
     along_proto = jnp.sum(proto_unit * proto_grad, axis=-1, keepdims=True)
     grad_protos = (proto_grad - proto_unit * along_proto) * proto_inverse
     loss_value = -loss_total / (2.0 * batch_row_count)

time: 804 us -> 628 us (0.78)
  waiting for transfers between devices: 388 us -> 229 us
  blocking collectives: 345 us -> 326 us
    psum x1, waiting for transfers between devices: 255 us -> 68.8 us  [body(): lax.psum((weight_part, loss_portion), 'mp')]
    reduce_scatter x1, waiting for transfers between devices: 0.02 us -> 66.1 us  [body(): lax.psum_scatter(jnp.einsum('bvk,kp->bvp', grad_half, proto_half, preferr...]
    psum x1, waiting for transfers between devices: 83.7 us -> 45.1 us  [body(): proto_grad = lax.psum(proto_grad, 'dp')]
    psum x1 -> x2, blocking collectives: 90.6 us -> 70.7 us  [the longest x1 53.6 us: body(): lax.psum(lax.psum((weight_part, loss_portion), 'mp'), 'dp')]
  transfers between devices with their start and end apart: 4 -> 4, of which waited for: 3 -> 4; matrix products, arithmetic and copies ran while one was open for 1% -> 1% of each run, Pallas kernels for 0% -> 0%
where the time goes in v1:
time: 628 us; the launch traced here: 626 us
  blocking collectives  326 us (52%)
  waiting for transfers between devices  229 us (36%)
  other arithmetic  33.2 us (5%)
  between operations  15.7 us (2%)
  matrix products  15.4 us (2%)
  local copies, waits for them, and re-layouts  6.56 us (1%)
    psum x3, blocking collectives, prototype_totals(): return lax.psum(jnp.sum(values, axis=0), 'dp')  170 us
    psum x3, blocking collectives, code_totals(): return lax.psum(jnp.sum(values, axis=-1), 'mp')  84.6 us
    psum x1, waiting for transfers between devices, body(): lax.psum((weight_part, loss_portion), 'mp')  68.8 us
    reduce_scatter x1, waiting for transfers between devices, body(): lax.psum_scatter(jnp.einsum('bvk,kp->bvp', grad_half, proto_half, preferr...  66.1 us
    psum x1, blocking collectives, body(): lax.psum(lax.psum((weight_part, loss_portion), 'mp'), 'dp')  53.6 us
    all_gather x1, waiting for transfers between devices, body(): all_embed = lax.all_gather(embed_half, 'mp', axis=0, tiled=True)  49.1 us
    psum x1, waiting for transfers between devices, body(): proto_grad = lax.psum(proto_grad, 'dp')  45.1 us
    psum x1, blocking collectives, body(): lax.psum((weight_part, loss_portion), 'mp')  17 us
  transfers between devices with their start and end apart: 4, of which 4 were waited for; matrix products, arithmetic and copies ran while one was open for 1% of the time, Pallas kernels for 0%

profile of v1, /device:TPU:2, one launch (start us, length us, event | category | flops | bytes accessed | tf_op | source)
XLA Modules:
  0.0 625.8 jit_solution(4891146653210776559)
XLA Ops:
  7.2 0.0 copy-start
  7.2 0.0 all-gather.2.cloned.1.call-start
  7.2 1.4 constant_dynamic-slice_fusion
  8.7 0.0 copy-start.5
  8.7 0.8 copy-done.5
  9.5 0.0 copy-done
  9.5 0.4 multiply_reduce_fusion.1
  9.8 0.0 copy-start.4
  9.9 0.8 copy-done.4
  10.6 0.7 multiply_convert_fusion.1
  11.4 0.0 all-gather.2.cloned.1.call-update
  11.4 0.0 reduce-scatter.2.cloned.1.call-start
  11.5 1.1 multiply_reduce_fusion.4
  12.6 49.1 %all-gather.2.cloned.1.call-done = bf16[2048,2,256]{0,2,1:T(8,128)(2,1)} async-done(((bf16[256,2,256]{0,2,1:T(8,128)(2,1)}), bf16[2048,2,256]{0,2,1:T(8,128)(2,1)}) %all-gather.2.cloned.1.call-update) | async-done | bytes 2097168 | tf_op jit(solution)/shard_map/all_gather | solution.py:58
  61.7 5.4 fusion.12
  67.1 53.0 %psum.85 = f32[2,375]{1,0:T(2,128)S(1)} all-reduce(f32[2,375]{1,0:T(2,128)S(1)} %get-tuple-element.13), channel_id=1, replica_groups=mesh['dp'=32,'mp'=8] {'dp'}, use_global_device_ids=true, to_apply=%region_5.0 | all-reduce | flops 750 | bytes 6000 | tf_op jit(solution)/shard_map/psum | solution.py:19
  120.1 3.8 exponential_reduce_fusion
  123.9 29.9 %psum.86 = f32[2048,2]{0,1:T(2,128)S(1)} all-reduce(f32[2048,2]{0,1:T(2,128)S(1)} %get-tuple-element.4), channel_id=1, replica_groups=mesh['dp'=32,'mp'=8] {'mp'}, use_global_device_ids=true, to_apply=%region_7.0 | all-reduce | flops 4096 | bytes 32768 | tf_op jit(solution)/shard_map/psum | solution.py:23
  153.8 4.4 fusion.8
  158.2 54.7 %psum.87 = f32[2,375]{1,0:T(2,128)S(1)} all-reduce(f32[2,375]{1,0:T(2,128)S(1)} %fusion.8), channel_id=1, replica_groups=mesh['dp'=32,'mp'=8] {'dp'}, use_global_device_ids=true, to_apply=%region_9.0 | all-reduce | flops 750 | bytes 6000 | tf_op jit(solution)/shard_map/psum | solution.py:19
  212.9 3.7 fusion.9
  216.7 27.0 %psum.88 = f32[2048,2]{0,1:T(2,128)S(1)} all-reduce(f32[2048,2]{0,1:T(2,128)S(1)} %fusion.9), channel_id=1, replica_groups=mesh['dp'=32,'mp'=8] {'mp'}, use_global_device_ids=true, to_apply=%region_11.0 | all-reduce | flops 4096 | bytes 32768 | tf_op jit(solution)/shard_map/psum | solution.py:23
  243.7 3.9 fusion.10
  247.6 62.7 %psum.89 = f32[2,375]{1,0:T(2,128)S(1)} all-reduce(f32[2,375]{1,0:T(2,128)S(1)} %fusion.10), channel_id=1, replica_groups=mesh['dp'=32,'mp'=8] {'dp'}, use_global_device_ids=true, to_apply=%region_13.0 | all-reduce | flops 750 | bytes 6000 | tf_op jit(solution)/shard_map/psum | solution.py:19
  310.3 0.0 slice-start
  310.3 4.3 fusion.11
  314.6 27.7 %all-reduce.1 = (f32[2048,2]{0,1:T(2,128)S(1)}, f32[2048,2]{0,1:T(2,128)S(1)}) all-reduce(f32[2048,2]{0,1:T(2,128)S(1)} %fusion.11, f32[2048,2]{0,1:T(2,128)S(1)} %get-tuple-element.3), channel_id=1, replica_groups=mesh['dp'=32,'mp'=8] {'mp'}, use_global_device_ids=true, to_apply=%region_15.0 | all-reduce | flops 8192 | bytes 65536 | tf_op jit(solution)/shard_map/psum | solution.py:23
  342.3 0.0 slice-start.1
  342.3 5.1 fusion.7
  347.4 0.0 slice-done
  347.4 0.0 slice-done.1
  347.4 0.0 copy-start.3
  347.5 2.6 multiply_reduce_fusion
  350.0 0.0 copy-start.1
  350.0 1.6 copy-done.1
  351.7 0.0 copy-done.3
  351.7 3.3 fusion.28
  355.0 0.0 copy-start.2
  355.0 0.0 reduce-scatter.2.cloned.1.call-update
  355.1 0.0 all-reduce.5.cloned.1.call-start
  355.1 66.1 %reduce-scatter.2.cloned.1.call-done = f32[256,2,256]{0,2,1:T(8,128)} async-done(((f32[2048,2,256]{0,2,1:T(8,128)}), f32[256,2,256]{0,2,1:T(8,128)}) %reduce-scatter.2.cloned.1.call-update) | async-done | bytes 524304 | tf_op jit(solution)/shard_map/reduce_scatter | solution.py:77
  421.2 3.0 convolution_bitcast_fusion
  424.2 0.0 all-reduce.5.cloned.1.call-update
  424.2 0.0 all-reduce.7.cloned.1.call-start
  424.3 0.0 copy-done.2
  424.3 3.4 convolution_bitcast_fusion.1
  427.6 68.8 %all-reduce.5.cloned.1.call-done = f32[512,256]{1,0:T(8,128)} async-done(((f32[512,256]{1,0:T(8,128)}), f32[512,256]{1,0:T(8,128)}) %all-reduce.5.cloned.1.call-update) | async-done | bytes 524304 | tf_op jit(solution)/shard_map/psum | solution.py:84
  496.4 0.0 all-reduce.7.cloned.1.call-update
  496.5 17.0 %psum.94 = f32[]{:T(128)} all-reduce(f32[]{:T(128)} %get-tuple-element.9), channel_id=1, replica_groups=mesh['dp'=32,'mp'=8] {'mp'}, use_global_device_ids=true, to_apply=%region_23.0 | all-reduce | flops 1 | bytes 8 | tf_op jit(solution)/shard_map/psum | solution.py:84
  513.5 53.6 %psum.95 = f32[]{:T(128)} all-reduce(f32[]{:T(128)} %psum.94), channel_id=1, replica_groups=mesh['dp'=32,'mp'=8] {'dp'}, use_global_device_ids=true, to_apply=%region_24.0 | all-reduce | flops 1 | bytes 8 | tf_op jit(solution)/shard_map/psum | solution.py:84
  567.8 45.1 %all-reduce.7.cloned.1.call-done = (f32[375,256]{1,0:T(8,128)}, f32[512,256]{1,0:T(8,128)}) async-done(((f32[375,256]{1,0:T(8,128)}, f32[512,256]{1,0:T(8,128)}), (f32[375,256]{1,0:T(8,128)}, f32[512,256]{1,0:T(8,128)})) %all-reduce.7.cloned.1.call-update) | async-done | bytes 908304 | tf_op jit(solution)/shard_map/psum | solution.py:76
  612.9 1.3 multiply_reduce_fusion.3
  614.2 2.0 subtract_multiply_fusion
  616.2 1.9 copy.30
  (4 shorter events, 0.0 us)
Async XLA Ops:
  7.2 2.3 copy-start
  7.2 54.5 %all-gather.2.cloned.1.call-start = ((), (), s32[]{:S(2)}) async-start(), calls=%async_computation.1 | async-start | bytes 2359296 | tf_op jit(solution)/shard_map/all_gather | solution.py:58
  8.7 0.8 copy-start.5
  9.8 0.8 copy-start.4
  11.4 409.8 %reduce-scatter.2.cloned.1.call-start = ((), (), s32[]{:S(2)}) async-start(), calls=%async_computation.2 | async-start | bytes 4718592 | tf_op jit(solution)/shard_map/reduce_scatter | solution.py:77
  310.3 37.1 %slice-start = ((s8[6160384]{0:T(1024)(128)(4,1)}), s8[1966080]{0:T(1024)(128)(4,1)S(1)}, s32[]{:S(2)}) async-start(s8[6160384]{0:T(1024)(128)(4,1)} %bitcast.19), calls=%async_computation.5 | async-start | bytes 3932160
  342.3 5.1 slice-start.1
  347.4 4.2 copy-start.3
  350.0 1.6 copy-start.1
  355.0 69.2 %copy-start.2 = (bf16[2048,2,375]{0,2,1:T(8,128)(2,1)S(1)}, bf16[2048,2,375]{0,2,1:T(8,128)(2,1)}, u32[]{:S(2)}) copy-start(bf16[2048,2,375]{0,2,1:T(8,128)(2,1)} %copy-done.1) | copy-start | bytes 9216004
  355.1 141.4 %all-reduce.5.cloned.1.call-start = ((), (), s32[]{:S(2)}) async-start(), calls=%async_computation.3 | async-start | bytes 1048576 | tf_op jit(solution)/shard_map/psum | solution.py:84
  424.2 188.7 %all-reduce.7.cloned.1.call-start = ((), (), s32[]{:S(2)}) async-start(), calls=%async_computation.4 | async-start | bytes 1818624 | tf_op jit(solution)/shard_map/psum | solution.py:76
Sparse Core Ops, SparseCore 0:
  11.5 50.1 all-gather.1
  355.2 66.0 reduce-scatter.1
  424.3 72.0 all-reduce.4
  500.6 112.1 all-reduce.6
